TPU v7x, 256 devices: a whole 4x4x8 slice. The times are simulated.
256 devices in a mesh: section: 4 (over x), shard: 64 (over z, y, core).
Axes of the slice: x: 4, y: 4, z: 8, core: 2. Of those that a mesh axis runs over, the one named last changes fastest.
Arguments:
- voltages: bfloat16 [4, 2, 1024, 32768], P('section', None, 'shard'), may hold values from -30 to 30, as said below
- feed_gains: bfloat16 [2, 1024, 1024], P(None, 'shard'), may hold values from -6 to 6
- grid_index: int32 [1024], replicated, may hold values from 0 to 1023, each once
- decay_rates: float32 [1024], P('shard'), may hold values from 0.3 to 0.95
- delays: int32 [1024, 512], replicated, may hold values from 0 to 4095
Outputs:
- dedispersed: bfloat16 [4, 7, 512, 2, 1024], P('section', None, None, None, 'shard')
Inputs may be any that keep to these rules, and one draw needn't show every extreme that they name: Real sample voltages.
All inputs are finite; a program needn't handle non-finite values.
Results may differ from a plain program's by a relative error of at most 0.009.
Values may be sent and summed in bfloat16 or wider, within the bound.
A program may use at most 192 MiB of HBM per device.

v0:
```python
import math
import jax
import jax.numpy as jnp
import numpy as np
from jax import lax
from jax.sharding import PartitionSpec as P

POL = 2
GRID_X = 4
GRID_Y = 256
NSAMP = 2048
TDFT = 16
FEEDS = 1024
CHANS = 1024
MODF = 7


def carried_in(part, axis, combine, identity):
    place = lax.axis_index(axis)
    gathered = jax.tree.map(lambda a: lax.all_gather(a, axis), part)
    state = jax.tree.map(lambda a, e: jnp.zeros_like(a) + jnp.asarray(e, a.dtype), part, identity)

    def one(lap, state):
        return combine(
            state, jax.tree.map(lambda a: lax.dynamic_index_in_dim(a, lap, 0, False), gathered)
        )

    return lax.fori_loop(0, place, one, state)


def spectral_constant():
    row_index = np.arange(CHANS, dtype=np.int64)[:, None]
    col_index = np.arange(NSAMP, dtype=np.int64)[None, :]
    angles = np.float32(2.0 * math.pi / NSAMP) * (row_index * col_index % NSAMP).astype(np.float32)
    table = np.concatenate([np.cos(angles), -np.sin(angles)], 0).astype(np.float32)
    return jnp.asarray(table).astype(jnp.bfloat16)


def twiddle_table(length):
    row_index = jnp.arange(length, dtype=jnp.int32)[:, None]
    col_index = jnp.arange(length, dtype=jnp.int32)[None, :]
    angles = 2.0 * math.pi / length * (row_index * col_index % length).astype(jnp.float32)
    cosine = jnp.cos(angles)
    sine_part = jnp.sin(angles)
    return jnp.stack([jnp.stack([cosine, -sine_part], 1), jnp.stack([sine_part, cosine], 1)], 0)


def frame_table():
    frames = jnp.arange(TDFT, dtype=jnp.int32)[:, None]
    freqs = jnp.arange(1, MODF + 1, dtype=jnp.int32)[None, :]
    angles = 2.0 * math.pi / TDFT * (frames * freqs % TDFT).astype(jnp.float32)
    return jnp.concatenate([jnp.cos(angles), -jnp.sin(angles)], 1) / math.sqrt(TDFT)


def form_beams(transposed_block, feed_gains, cell_feed):
    chan_count = transposed_block.shape[1]
    pol_count = transposed_block.shape[2]
    values = transposed_block.reshape(2, chan_count, pol_count, FEEDS, TDFT).astype(jnp.float32)
    gain_values = feed_gains.astype(jnp.float32)[:, :, None, :, None]
    real_part = gain_values[0] * values[0] - gain_values[1] * values[1]
    imag_part = gain_values[0] * values[1] + gain_values[1] * values[0]
    calibrated = jnp.stack([real_part, imag_part]).astype(jnp.bfloat16)
    gridded = jnp.take(calibrated, cell_feed, axis=3).reshape(
        2, chan_count, pol_count, GRID_X, GRID_Y, TDFT
    )
    rows = twiddle_table(GRID_Y).astype(jnp.bfloat16)
    row_beams = jnp.einsum("acpxyn,aybw->bcpxwn", gridded, rows, preferred_element_type=jnp.float32)
    beam_voltage = jnp.einsum(
        "bcpxwn,bxeu->ecpnuw", row_beams, twiddle_table(GRID_X), precision=lax.Precision.HIGHEST
    )
    powers = jnp.sum(beam_voltage * beam_voltage, axis=0)
    return jnp.moveaxis(powers, 1, 0).reshape(pol_count, chan_count, TDFT, FEEDS)


def dedisperse(freq_major, delays):
    residues = delays % TDFT
    contract = (((0,), (0,)), ((), ()))

    def per_frequency(position_index):
        frequency = position_index + 1
        angles = 2.0 * math.pi / TDFT * (frequency * residues % TDFT).astype(jnp.float32)
        cosine_part = jnp.cos(angles).astype(jnp.bfloat16)
        sine_part = jnp.sin(angles).astype(jnp.bfloat16)
        mod_real = freq_major[position_index]
        mod_imag = freq_major[MODF + position_index]
        real_out = lax.dot_general(
            cosine_part, mod_real, contract, preferred_element_type=jnp.float32
        ) + lax.dot_general(sine_part, mod_imag, contract, preferred_element_type=jnp.float32)
        imag_out = lax.dot_general(
            cosine_part, mod_imag, contract, preferred_element_type=jnp.float32
        ) - lax.dot_general(sine_part, mod_real, contract, preferred_element_type=jnp.float32)
        result = jnp.stack([real_out, imag_out], 1) / math.sqrt(CHANS)
        return result.astype(jnp.bfloat16)

    return lax.map(per_frequency, jnp.arange(MODF, dtype=jnp.int32))


def combine(earlier, later):
    return (
        earlier[0] * later[0],
        later[0] * earlier[1] + later[1],
        later[0] * earlier[2] + later[2],
    )


def shards(voltages, feed_gains, grid_index, decay_rates, delays):
    cell_feed = (
        jnp.zeros((FEEDS,), jnp.int32).at[grid_index].set(jnp.arange(FEEDS, dtype=jnp.int32))
    )
    local_feeds = voltages.shape[2]
    samples = voltages[0].reshape(POL * local_feeds * TDFT, NSAMP)
    spectra = lax.dot_general(
        spectral_constant(), samples, (((1,), (1,)), ((), ())), preferred_element_type=jnp.float32
    )
    spectra = (
        (spectra * (1.0 / math.sqrt(NSAMP)))
        .astype(jnp.bfloat16)
        .reshape(2, CHANS, POL, local_feeds * TDFT)
    )
    turned = lax.all_to_all(spectra, "shard", split_axis=1, concat_axis=3, tiled=True)
    per_pol = form_beams(turned, feed_gains, cell_feed)
    beam_power = jnp.sum(per_pol, axis=0)
    levels = jnp.mean(beam_power, axis=(1, 2)) + 1e-06
    unity = jnp.ones_like(levels)
    nothing = jnp.zeros_like(levels)
    prefix = carried_in((decay_rates, levels, unity), "section", combine, (unity, nothing, nothing))
    baseline_level = (decay_rates * prefix[1] + levels) / (decay_rates * prefix[2] + 1.0)
    normalized = beam_power / baseline_level[:, None, None] - 1.0
    modulated = jnp.einsum(
        "cnb,nq->cbq", normalized, frame_table(), precision=lax.Precision.HIGHEST
    ).astype(jnp.bfloat16)
    flattened = modulated.reshape(modulated.shape[0], FEEDS * 2 * MODF)
    moved = lax.all_to_all(flattened, "shard", split_axis=1, concat_axis=0, tiled=True)
    local_beams = FEEDS // lax.axis_size("shard")
    gathered = moved.reshape(CHANS, local_beams, 2 * MODF)
    freq_major = jnp.transpose(gathered, (2, 0, 1))
    return dedisperse(freq_major, delays)[None]


def solution(mesh):
    in_specs = (P("section", None, "shard", None), P(None, "shard", None), P(), P("shard"), P())
    out_specs = P("section", None, None, None, "shard")
    return jax.shard_map(shards, mesh=mesh, in_specs=in_specs, out_specs=out_specs, check_vma=False)
```

profile of v0, /device:TPU:1, one launch (start us, length us, event | category | flops | bytes accessed | tf_op | source)
XLA Modules:
  0.0 509.6 jit_solution(17534313984835223672)
XLA Ops:
  2.9 9.2 %multiply_convert_fusion = bf16[2048,512]{1,0:T(8,128)(2,1)} fusion(bf16[2048,2048]{1,0:T(8,128)(2,1)} %constant.189, bf16[512,2048]{1,0:T(8,128)(2,1)S(1)} %reshape_squeeze.3), kind=kOutput, calls=%fused_computation.43 | convolution fusion | flops 4297064448 | bytes 12582912 | tf_op jit(solution)/shard_map/dot_general | solution.py:112
  17.4 13.3 %all-to-all-start = ((bf16[2,1024,2,256]{3,2,0,1:T(2,128)(2,1)}), bf16[2,1024,2,256]{3,2,0,1:T(2,128)(2,1)S(1)}, u32[]{:S(2)}, u32[]{:S(2)}) async-start(bf16[2,1024,2,256]{3,2,0,1:T(2,128)(2,1)} %copy.40), calls=%async_computation | async-start | bytes 4194304 | tf_op jit(solution)/shard_map/all_to_all | solution.py:120
  30.8 4.8 scatter_custom_fusion
  40.5 39.9 %all-to-all-done = bf16[2,1024,2,256]{3,2,0,1:T(2,128)(2,1)S(1)} async-done(((bf16[2,1024,2,256]{3,2,0,1:T(2,128)(2,1)}), bf16[2,1024,2,256]{3,2,0,1:T(2,128)(2,1)S(1)}, u32[]{:S(2)}, u32[]{:S(2)}) %all-to-all-start) | async-done | bytes 2097184 | tf_op jit(solution)/shard_map/all_to_all | solution.py:120
  84.5 8.6 %slice.26 = f32[1,16,2,1024,16]{4,3,2,1,0:T(8,128)} reshape(f32[1,16,2,64,256]{4,3,2,1,0:T(8,128)S(1)} %copy.42) | data formatting | bytes 4194304 | tf_op jit(solution)/shard_map/slice | solution.py:60
  95.9 8.6 %slice.29 = f32[1,16,2,1024,16]{4,3,2,1,0:T(8,128)} reshape(f32[1,16,2,64,256]{4,3,2,1,0:T(8,128)S(1)} %copy.43) | data formatting | bytes 4194304 | tf_op jit(solution)/shard_map/slice | solution.py:60
  104.5 18.1 %multiply_subtract_fusion = (bf16[1,16,2,1024,16]{4,3,2,1,0:T(8,128)(2,1)}, bf16[1,16,2,1024,16]{4,3,2,1,0:T(8,128)(2,1)}) fusion(f32[1,16,2,1024,16]{4,3,2,1,0:T(8,128)} %slice.29, f32[1,16,2,1024,16]{4,3,2,1,0:T(8,128)} %slice.26, f32[16,1024]{1,0:T(8,128)S(1)} %get-tuple-element.203, f32[16,1024]{1,0:T(8,128)S(1)} %get-tuple-element.202), kind=kLoop, calls=%fused_computation.37 | loop fusion | flops 4194304 | bytes 6422528 | tf_op jit(solution)/shard_map/sub | solution.py:60
  122.5 6.7 %copy.44 = bf16[1,16,2,1024,16]{3,4,2,1,0:T(8,128)(2,1)S(1)} copy(bf16[1,16,2,1024,16]{4,3,2,1,0:T(8,128)(2,1)} %get-tuple-element.196) | data formatting | bytes 2097152 | tf_op jit(solution)/shard_map/sub | solution.py:60
  129.2 7.8 %copy.45 = bf16[1,16,2,1024,16]{3,4,2,1,0:T(8,128)(2,1)} copy(bf16[1,16,2,1024,16]{4,3,2,1,0:T(8,128)(2,1)} %get-tuple-element.197) | data formatting | bytes 2097152 | tf_op jit(solution)/shard_map/add | solution.py:61
  138.4 16.1 %copy.46 = bf16[2,16,2,1024,16]{4,1,3,2,0:T(8,128)(2,1)} copy(bf16[2,16,2,1024,16]{3,4,2,1,0:T(8,128)(2,1)S(1)} %pad_maximum_fusion) | data formatting | bytes 4194304 | tf_op jit(solution)/shard_map/stack | solution.py:62
  154.5 20.1 %gather_fusion = bf16[1024,2,16,2,16]{4,2,3,1,0:T(8,128)(2,1)} fusion(bf16[2,16,2,1024,16]{4,1,3,2,0:T(8,128)(2,1)} %copy.46, s32[1024]{0:T(1024)S(1)} %fusion.59), kind=kCustom, calls=%fused_computation | custom fusion | bytes 4198400 | tf_op jit(solution)/shard_map/jit(_take)/gather | solution.py:63
  174.7 17.1 %copy.47 = bf16[2,16,2,4,256,16]{4,5,0,3,2,1:T(8,128)(2,1)S(1)} copy(bf16[2,16,2,4,256,16]{5,1,2,0,4,3:T(8,128)(2,1)} %bitcast.111) | data formatting | bytes 4194304 | tf_op jit(solution)/shard_map/jit(_take)/gather | solution.py:63
  193.0 12.1 %fusion.25 = (f32[16]{0:T(128)S(1)}, f32[4,16,256,16]{2,0,3,1:T(4,128)S(1)}) fusion(f32[2,16,2,4,256,16]{4,5,3,2,1,0:T(8,128)S(1)} %convolution_bitcast_fusion, f32[1,4,2,4]{1,3,0,2:T(4,128)S(1)} %copy.38, f32[1,4,2,4]{1,3,0,2:T(4,128)S(1)} %copy.37), kind=kOutput, calls=%fused_computation.44 | convolution fusion | flops 103546928 | bytes 5243200 | tf_op jit(solution)/shard_map/bcpxwn,bxeu->ecpnuw/dot_general | solution.py:68
  205.3 8.4 %all-reduce.2 = (f32[64]{0:T(128)S(1)}, f32[64]{0:T(128)S(1)}) all-reduce(f32[64]{0:T(128)S(1)} %dynamic-update-slice, f32[64]{0:T(128)S(1)} %fusion.69), channel_id=2, replica_groups=mesh['section'=4,'shard'=64] {'section'}, use_global_device_ids=true, to_apply=%add | all-reduce | flops 128 | bytes 1024
  218.9 5.8 %all_to_all.20 = bf16[16,64,224]{2,1,0:T(8,128)(2,1)S(1)} reshape(bf16[16,1024,14]{2,1,0:T(8,128)(2,1)} %copy.49) | data formatting | bytes 917504 | tf_op jit(solution)/shard_map/all_to_all | solution.py:133
  225.9 9.0 %all-to-all-start.1 = ((bf16[16,64,224]{2,0,1:T(8,128)(2,1)}), bf16[16,64,224]{2,0,1:T(8,128)(2,1)S(1)}, u32[]{:S(2)}, u32[]{:S(2)}) async-start(bf16[16,64,224]{2,0,1:T(8,128)(2,1)} %copy.50), calls=%async_computation.1 | async-start | bytes 1048576 | tf_op jit(solution)/shard_map/all_to_all | solution.py:133
  236.9 15.6 %all-to-all-done.1 = bf16[16,64,224]{2,0,1:T(8,128)(2,1)S(1)} async-done(((bf16[16,64,224]{2,0,1:T(8,128)(2,1)}), bf16[16,64,224]{2,0,1:T(8,128)(2,1)S(1)}, u32[]{:S(2)}, u32[]{:S(2)}) %all-to-all-start.1) | async-done | bytes 458784 | tf_op jit(solution)/shard_map/all_to_all | solution.py:133
  252.6 3.3 copy.51
  255.9 6.7 %reshape.246 = bf16[1024,16,14]{0,2,1:T(8,128)(2,1)S(1)} reshape(bf16[64,16,224]{1,0,2:T(8,128)(2,1)} %copy.51) | data formatting | bytes 917504 | tf_op jit(solution)/shard_map/reshape | solution.py:135
  262.8 246.6 %while.28 = (s32[]{:T(128)}, bf16[7,512,2,16]{1,3,2,0:T(8,128)(2,1)}, s32[7]{0:T(128)S(1)}, s32[1024,512]{1,0:T(8,128)}, bf16[14,1024,16]{1,2,0:T(8,128)(2,1)S(1...) while((s32[]{:T(128)}, bf16[7,512,2,16]{1,3,2,0:T(8,128)(2,1)}, s32[7]{0:T(128)S(1)}, ...), condition=%wide.region_6.7_spmd, body=%wide.region_5.6_spmd.sunk | while | flops 76611592 | bytes 13009633 | solution.py:95
  268.8 6.9 %fusion.98 = f32[512,16]{0,1:T(8,128)S(1)} fusion(f32[1024,512]{1,0:T(8,128)S(1)} %fusion.95, bf16[14,1024,16]{1,2,0:T(8,128)(2,1)S(1)} %get-tuple-element.336, s32[]{:T(128)S(6)} %select_n.175), kind=kOutput, calls=%fused_computation.19.clone.1 | convolution fusion | flops 17301504 | bytes 2162692 | tf_op jit(solution)/shard_map/while/body/eval_jaxpr/dot_general | solution.py:86
  276.9 6.9 %fusion.99 = f32[1,512,1,16]{1,3,2,0:T(8,128)S(1)} fusion(f32[512,16]{0,1:T(8,128)S(1)} %fusion.98, f32[1024,512]{1,0:T(8,128)S(1)} %fusion.95, bf16[14,1024,16]{1,2,0:T(8,128)(2,1)S(1)} %get-tuple-element.336, s32[]{:T(128)S(6)} %select_n.174), kind=kOutput, calls=%fused_computation.18.clone.1 | convolution fusion | flops 17309696 | bytes 2195460 | tf_op jit(solution)/shard_map/while/body/eval_jaxpr/dot_general | solution.py:88
  283.9 6.9 %fusion.96 = f32[512,16]{0,1:T(8,128)S(1)} fusion(f32[1024,512]{1,0:T(8,128)S(1)} %fusion.95, bf16[14,1024,16]{1,2,0:T(8,128)(2,1)S(1)} %get-tuple-element.336, s32[]{:T(128)S(6)} %select_n.174), kind=kOutput, calls=%fused_computation.20.clone.1 | convolution fusion | flops 17301504 | bytes 2162692 | tf_op jit(solution)/shard_map/while/body/eval_jaxpr/dot_general | solution.py:89
  290.7 6.9 %fusion.97 = f32[1,512,1,16]{1,3,2,0:T(8,128)S(1)} fusion(f32[512,16]{0,1:T(8,128)S(1)} %fusion.96, f32[1024,512]{1,0:T(8,128)S(1)} %fusion.95, bf16[14,1024,16]{1,2,0:T(8,128)(2,1)S(1)} %get-tuple-element.336, s32[]{:T(128)S(6)} %select_n.175), kind=kOutput, calls=%fused_computation.16.clone.1 | convolution fusion | flops 17309696 | bytes 2195460 | tf_op jit(solution)/shard_map/while/body/eval_jaxpr/dot_general | solution.py:91
  304.0 6.9 %fusion.98 = f32[512,16]{0,1:T(8,128)S(1)} fusion(f32[1024,512]{1,0:T(8,128)S(1)} %fusion.95, bf16[14,1024,16]{1,2,0:T(8,128)(2,1)S(1)} %get-tuple-element.336, s32[]{:T(128)S(6)} %select_n.175), kind=kOutput, calls=%fused_computation.19.clone.1 | convolution fusion | flops 17301504 | bytes 2162692 | tf_op jit(solution)/shard_map/while/body/eval_jaxpr/dot_general | solution.py:86
  312.1 6.9 %fusion.99 = f32[1,512,1,16]{1,3,2,0:T(8,128)S(1)} fusion(f32[512,16]{0,1:T(8,128)S(1)} %fusion.98, f32[1024,512]{1,0:T(8,128)S(1)} %fusion.95, bf16[14,1024,16]{1,2,0:T(8,128)(2,1)S(1)} %get-tuple-element.336, s32[]{:T(128)S(6)} %select_n.174), kind=kOutput, calls=%fused_computation.18.clone.1 | convolution fusion | flops 17309696 | bytes 2195460 | tf_op jit(solution)/shard_map/while/body/eval_jaxpr/dot_general | solution.py:88
  319.1 6.9 %fusion.96 = f32[512,16]{0,1:T(8,128)S(1)} fusion(f32[1024,512]{1,0:T(8,128)S(1)} %fusion.95, bf16[14,1024,16]{1,2,0:T(8,128)(2,1)S(1)} %get-tuple-element.336, s32[]{:T(128)S(6)} %select_n.174), kind=kOutput, calls=%fused_computation.20.clone.1 | convolution fusion | flops 17301504 | bytes 2162692 | tf_op jit(solution)/shard_map/while/body/eval_jaxpr/dot_general | solution.py:89
  325.9 6.9 %fusion.97 = f32[1,512,1,16]{1,3,2,0:T(8,128)S(1)} fusion(f32[512,16]{0,1:T(8,128)S(1)} %fusion.96, f32[1024,512]{1,0:T(8,128)S(1)} %fusion.95, bf16[14,1024,16]{1,2,0:T(8,128)(2,1)S(1)} %get-tuple-element.336, s32[]{:T(128)S(6)} %select_n.175), kind=kOutput, calls=%fused_computation.16.clone.1 | convolution fusion | flops 17309696 | bytes 2195460 | tf_op jit(solution)/shard_map/while/body/eval_jaxpr/dot_general | solution.py:91
  339.2 6.9 %fusion.98 = f32[512,16]{0,1:T(8,128)S(1)} fusion(f32[1024,512]{1,0:T(8,128)S(1)} %fusion.95, bf16[14,1024,16]{1,2,0:T(8,128)(2,1)S(1)} %get-tuple-element.336, s32[]{:T(128)S(6)} %select_n.175), kind=kOutput, calls=%fused_computation.19.clone.1 | convolution fusion | flops 17301504 | bytes 2162692 | tf_op jit(solution)/shard_map/while/body/eval_jaxpr/dot_general | solution.py:86
  347.3 6.9 %fusion.99 = f32[1,512,1,16]{1,3,2,0:T(8,128)S(1)} fusion(f32[512,16]{0,1:T(8,128)S(1)} %fusion.98, f32[1024,512]{1,0:T(8,128)S(1)} %fusion.95, bf16[14,1024,16]{1,2,0:T(8,128)(2,1)S(1)} %get-tuple-element.336, s32[]{:T(128)S(6)} %select_n.174), kind=kOutput, calls=%fused_computation.18.clone.1 | convolution fusion | flops 17309696 | bytes 2195460 | tf_op jit(solution)/shard_map/while/body/eval_jaxpr/dot_general | solution.py:88
  354.2 6.9 %fusion.96 = f32[512,16]{0,1:T(8,128)S(1)} fusion(f32[1024,512]{1,0:T(8,128)S(1)} %fusion.95, bf16[14,1024,16]{1,2,0:T(8,128)(2,1)S(1)} %get-tuple-element.336, s32[]{:T(128)S(6)} %select_n.174), kind=kOutput, calls=%fused_computation.20.clone.1 | convolution fusion | flops 17301504 | bytes 2162692 | tf_op jit(solution)/shard_map/while/body/eval_jaxpr/dot_general | solution.py:89
  361.1 6.9 %fusion.97 = f32[1,512,1,16]{1,3,2,0:T(8,128)S(1)} fusion(f32[512,16]{0,1:T(8,128)S(1)} %fusion.96, f32[1024,512]{1,0:T(8,128)S(1)} %fusion.95, bf16[14,1024,16]{1,2,0:T(8,128)(2,1)S(1)} %get-tuple-element.336, s32[]{:T(128)S(6)} %select_n.175), kind=kOutput, calls=%fused_computation.16.clone.1 | convolution fusion | flops 17309696 | bytes 2195460 | tf_op jit(solution)/shard_map/while/body/eval_jaxpr/dot_general | solution.py:91
  374.3 6.9 %fusion.98 = f32[512,16]{0,1:T(8,128)S(1)} fusion(f32[1024,512]{1,0:T(8,128)S(1)} %fusion.95, bf16[14,1024,16]{1,2,0:T(8,128)(2,1)S(1)} %get-tuple-element.336, s32[]{:T(128)S(6)} %select_n.175), kind=kOutput, calls=%fused_computation.19.clone.1 | convolution fusion | flops 17301504 | bytes 2162692 | tf_op jit(solution)/shard_map/while/body/eval_jaxpr/dot_general | solution.py:86
  382.5 6.9 %fusion.99 = f32[1,512,1,16]{1,3,2,0:T(8,128)S(1)} fusion(f32[512,16]{0,1:T(8,128)S(1)} %fusion.98, f32[1024,512]{1,0:T(8,128)S(1)} %fusion.95, bf16[14,1024,16]{1,2,0:T(8,128)(2,1)S(1)} %get-tuple-element.336, s32[]{:T(128)S(6)} %select_n.174), kind=kOutput, calls=%fused_computation.18.clone.1 | convolution fusion | flops 17309696 | bytes 2195460 | tf_op jit(solution)/shard_map/while/body/eval_jaxpr/dot_general | solution.py:88
  389.4 6.9 %fusion.96 = f32[512,16]{0,1:T(8,128)S(1)} fusion(f32[1024,512]{1,0:T(8,128)S(1)} %fusion.95, bf16[14,1024,16]{1,2,0:T(8,128)(2,1)S(1)} %get-tuple-element.336, s32[]{:T(128)S(6)} %select_n.174), kind=kOutput, calls=%fused_computation.20.clone.1 | convolution fusion | flops 17301504 | bytes 2162692 | tf_op jit(solution)/shard_map/while/body/eval_jaxpr/dot_general | solution.py:89
  396.3 6.9 %fusion.97 = f32[1,512,1,16]{1,3,2,0:T(8,128)S(1)} fusion(f32[512,16]{0,1:T(8,128)S(1)} %fusion.96, f32[1024,512]{1,0:T(8,128)S(1)} %fusion.95, bf16[14,1024,16]{1,2,0:T(8,128)(2,1)S(1)} %get-tuple-element.336, s32[]{:T(128)S(6)} %select_n.175), kind=kOutput, calls=%fused_computation.16.clone.1 | convolution fusion | flops 17309696 | bytes 2195460 | tf_op jit(solution)/shard_map/while/body/eval_jaxpr/dot_general | solution.py:91
  409.5 6.9 %fusion.98 = f32[512,16]{0,1:T(8,128)S(1)} fusion(f32[1024,512]{1,0:T(8,128)S(1)} %fusion.95, bf16[14,1024,16]{1,2,0:T(8,128)(2,1)S(1)} %get-tuple-element.336, s32[]{:T(128)S(6)} %select_n.175), kind=kOutput, calls=%fused_computation.19.clone.1 | convolution fusion | flops 17301504 | bytes 2162692 | tf_op jit(solution)/shard_map/while/body/eval_jaxpr/dot_general | solution.py:86
  417.7 6.9 %fusion.99 = f32[1,512,1,16]{1,3,2,0:T(8,128)S(1)} fusion(f32[512,16]{0,1:T(8,128)S(1)} %fusion.98, f32[1024,512]{1,0:T(8,128)S(1)} %fusion.95, bf16[14,1024,16]{1,2,0:T(8,128)(2,1)S(1)} %get-tuple-element.336, s32[]{:T(128)S(6)} %select_n.174), kind=kOutput, calls=%fused_computation.18.clone.1 | convolution fusion | flops 17309696 | bytes 2195460 | tf_op jit(solution)/shard_map/while/body/eval_jaxpr/dot_general | solution.py:88
  424.6 6.9 %fusion.96 = f32[512,16]{0,1:T(8,128)S(1)} fusion(f32[1024,512]{1,0:T(8,128)S(1)} %fusion.95, bf16[14,1024,16]{1,2,0:T(8,128)(2,1)S(1)} %get-tuple-element.336, s32[]{:T(128)S(6)} %select_n.174), kind=kOutput, calls=%fused_computation.20.clone.1 | convolution fusion | flops 17301504 | bytes 2162692 | tf_op jit(solution)/shard_map/while/body/eval_jaxpr/dot_general | solution.py:89
  431.5 6.9 %fusion.97 = f32[1,512,1,16]{1,3,2,0:T(8,128)S(1)} fusion(f32[512,16]{0,1:T(8,128)S(1)} %fusion.96, f32[1024,512]{1,0:T(8,128)S(1)} %fusion.95, bf16[14,1024,16]{1,2,0:T(8,128)(2,1)S(1)} %get-tuple-element.336, s32[]{:T(128)S(6)} %select_n.175), kind=kOutput, calls=%fused_computation.16.clone.1 | convolution fusion | flops 17309696 | bytes 2195460 | tf_op jit(solution)/shard_map/while/body/eval_jaxpr/dot_general | solution.py:91
  444.7 6.9 %fusion.98 = f32[512,16]{0,1:T(8,128)S(1)} fusion(f32[1024,512]{1,0:T(8,128)S(1)} %fusion.95, bf16[14,1024,16]{1,2,0:T(8,128)(2,1)S(1)} %get-tuple-element.336, s32[]{:T(128)S(6)} %select_n.175), kind=kOutput, calls=%fused_computation.19.clone.1 | convolution fusion | flops 17301504 | bytes 2162692 | tf_op jit(solution)/shard_map/while/body/eval_jaxpr/dot_general | solution.py:86
  452.9 6.9 %fusion.99 = f32[1,512,1,16]{1,3,2,0:T(8,128)S(1)} fusion(f32[512,16]{0,1:T(8,128)S(1)} %fusion.98, f32[1024,512]{1,0:T(8,128)S(1)} %fusion.95, bf16[14,1024,16]{1,2,0:T(8,128)(2,1)S(1)} %get-tuple-element.336, s32[]{:T(128)S(6)} %select_n.174), kind=kOutput, calls=%fused_computation.18.clone.1 | convolution fusion | flops 17309696 | bytes 2195460 | tf_op jit(solution)/shard_map/while/body/eval_jaxpr/dot_general | solution.py:88
  459.8 6.9 %fusion.96 = f32[512,16]{0,1:T(8,128)S(1)} fusion(f32[1024,512]{1,0:T(8,128)S(1)} %fusion.95, bf16[14,1024,16]{1,2,0:T(8,128)(2,1)S(1)} %get-tuple-element.336, s32[]{:T(128)S(6)} %select_n.174), kind=kOutput, calls=%fused_computation.20.clone.1 | convolution fusion | flops 17301504 | bytes 2162692 | tf_op jit(solution)/shard_map/while/body/eval_jaxpr/dot_general | solution.py:89
  466.7 6.9 %fusion.97 = f32[1,512,1,16]{1,3,2,0:T(8,128)S(1)} fusion(f32[512,16]{0,1:T(8,128)S(1)} %fusion.96, f32[1024,512]{1,0:T(8,128)S(1)} %fusion.95, bf16[14,1024,16]{1,2,0:T(8,128)(2,1)S(1)} %get-tuple-element.336, s32[]{:T(128)S(6)} %select_n.175), kind=kOutput, calls=%fused_computation.16.clone.1 | convolution fusion | flops 17309696 | bytes 2195460 | tf_op jit(solution)/shard_map/while/body/eval_jaxpr/dot_general | solution.py:91
  479.9 6.9 %fusion.98 = f32[512,16]{0,1:T(8,128)S(1)} fusion(f32[1024,512]{1,0:T(8,128)S(1)} %fusion.95, bf16[14,1024,16]{1,2,0:T(8,128)(2,1)S(1)} %get-tuple-element.336, s32[]{:T(128)S(6)} %select_n.175), kind=kOutput, calls=%fused_computation.19.clone.1 | convolution fusion | flops 17301504 | bytes 2162692 | tf_op jit(solution)/shard_map/while/body/eval_jaxpr/dot_general | solution.py:86
  488.1 6.9 %fusion.99 = f32[1,512,1,16]{1,3,2,0:T(8,128)S(1)} fusion(f32[512,16]{0,1:T(8,128)S(1)} %fusion.98, f32[1024,512]{1,0:T(8,128)S(1)} %fusion.95, bf16[14,1024,16]{1,2,0:T(8,128)(2,1)S(1)} %get-tuple-element.336, s32[]{:T(128)S(6)} %select_n.174), kind=kOutput, calls=%fused_computation.18.clone.1 | convolution fusion | flops 17309696 | bytes 2195460 | tf_op jit(solution)/shard_map/while/body/eval_jaxpr/dot_general | solution.py:88
  495.0 6.9 %fusion.96 = f32[512,16]{0,1:T(8,128)S(1)} fusion(f32[1024,512]{1,0:T(8,128)S(1)} %fusion.95, bf16[14,1024,16]{1,2,0:T(8,128)(2,1)S(1)} %get-tuple-element.336, s32[]{:T(128)S(6)} %select_n.174), kind=kOutput, calls=%fused_computation.20.clone.1 | convolution fusion | flops 17301504 | bytes 2162692 | tf_op jit(solution)/shard_map/while/body/eval_jaxpr/dot_general | solution.py:89
  501.9 6.9 %fusion.97 = f32[1,512,1,16]{1,3,2,0:T(8,128)S(1)} fusion(f32[512,16]{0,1:T(8,128)S(1)} %fusion.96, f32[1024,512]{1,0:T(8,128)S(1)} %fusion.95, bf16[14,1024,16]{1,2,0:T(8,128)(2,1)S(1)} %get-tuple-element.336, s32[]{:T(128)S(6)} %select_n.175), kind=kOutput, calls=%fused_computation.16.clone.1 | convolution fusion | flops 17309696 | bytes 2195460 | tf_op jit(solution)/shard_map/while/body/eval_jaxpr/dot_general | solution.py:91
  (79 shorter events, 57.2 us)
Async XLA Ops:
  17.4 13.3 %copy-start.2 = (bf16[2,16,1024]{2,1,0:T(8,128)(2,1)S(1)}, bf16[2,16,1024]{2,1,0:T(8,128)(2,1)}, u32[]{:S(2)}) copy-start(bf16[2,16,1024]{2,1,0:T(8,128)(2,1)} %param.11) | copy-start | bytes 196612
  17.4 13.3 %copy-start.3 = (s32[1024]{0:T(1024)S(1)}, s32[1024]{0:T(1024)}, u32[]{:S(2)}) copy-start(s32[1024]{0:T(1024)} %param.12) | copy-start | bytes 12292
  17.4 18.5 %copy-start.5 = (u32[256]{0:T(256)S(1)}, u32[256]{0:T(256)}, u32[]{:S(2)}) copy-start(u32[256]{0:T(256)} %constant.192) | copy-start | bytes 3076
  17.4 19.9 %copy-start.4 = (f32[16]{0:T(128)S(1)}, f32[16]{0:T(128)}, u32[]{:S(2)}) copy-start(f32[16]{0:T(128)} %param.13) | copy-start | bytes 196
  17.4 63.0 %all-to-all-start = ((bf16[2,1024,2,256]{3,2,0,1:T(2,128)(2,1)}), bf16[2,1024,2,256]{3,2,0,1:T(2,128)(2,1)S(1)}, u32[]{:S(2)}, u32[]{:S(2)}) async-start(bf16[2,1024,2,256]{3,2,0,1:T(2,128)(2,1)} %copy.40), calls=%async_computation | async-start | bytes 4194304 | tf_op jit(solution)/shard_map/all_to_all | solution.py:120
  174.6 17.1 %copy-start.1 = (bf16[1,256,2,256]{3,1,0,2:T(8,128)(2,1)S(1)}, bf16[1,256,2,256]{3,1,0,2:T(8,128)(2,1)}, u32[]{:S(2)}) copy-start(bf16[1,256,2,256]{3,1,0,2:T(8,128)(2,1)} %get-tuple-element.201) | copy-start | bytes 786436
  224.8 10.1 %copy-start = (s32[1024,512]{1,0:T(8,128)S(1)}, s32[1024,512]{1,0:T(8,128)}, u32[]{:S(2)}) copy-start(s32[1024,512]{1,0:T(8,128)} %param.14) | copy-start | bytes 6291460
  225.9 26.7 %all-to-all-start.1 = ((bf16[16,64,224]{2,0,1:T(8,128)(2,1)}), bf16[16,64,224]{2,0,1:T(8,128)(2,1)S(1)}, u32[]{:S(2)}, u32[]{:S(2)}) async-start(bf16[16,64,224]{2,0,1:T(8,128)(2,1)} %copy.50), calls=%async_computation.1 | async-start | bytes 1048576 | tf_op jit(solution)/shard_map/all_to_all | solution.py:133
where the time goes:
time: 516 us; the launch traced here: 510 us
  matrix products  217 us (42%)
  local copies, waits for them, and re-layouts  131 us (25%)
  waiting for transfers between devices  55.5 us (11%)
  other arithmetic  47.6 us (9%)
  loops' own time  27.1 us (5%)
  starting transfers between devices  22.3 us (4%)
  blocking collectives  8.44 us (2%)
    dot_general x7, matrix products, per_frequency(): lax.dot_general(sine_part, mod_imag, contract, preferred_element_type=jnp...  48.5 us
    dot_general x7, matrix products, per_frequency(): lax.dot_general(sine_part, mod_real, contract, preferred_element_type=jnp...  48.4 us
    dot_general x7, matrix products, per_frequency(): lax.dot_general(cosine_part, mod_real, contract, preferred_element_type=j...  48.1 us
    dot_general x7, matrix products, per_frequency(): lax.dot_general(cosine_part, mod_imag, contract, preferred_element_type=j...  48 us
    all_to_all x1, waiting for transfers between devices, shards(): lax.all_to_all(spectra, 'shard', split_axis=1, concat_axis=3, tiled=True)  39.9 us
    gather x2, local copies, waits for them, and re-layouts, form_beams(): jnp.take(calibrated, cell_feed, axis=3)  37.3 us
    another operation x1, loops' own time, dedisperse(): return lax.map(per_frequency, jnp.arange(MODF, dtype=jnp.int32))  27.1 us
    slice x5, local copies, waits for them, and re-layouts, form_beams(): real_part = gain_values[0] * values[0] - gain_values[1] * values[1]  23.2 us
  transfers between devices with their start and end apart: 2, of which 2 were waited for; matrix products, arithmetic and copies ran while one was open for 2% of the time, Pallas kernels for 0%

commit v1 on v0

--- a/solution.py
+++ b/solution.py
@@ -13,6 +13,13 @@
 FEEDS = 1024
 CHANS = 1024
 MODF = 7
+
+
+def trade_parts(value, axis, split, join):
+    size = lax.axis_size(axis)
+    blocks = jnp.stack(jnp.split(value, size, axis=split), axis=0)
+    blocks = lax.all_to_all(blocks, axis, split_axis=0, concat_axis=0)
+    return jnp.concatenate(blocks, axis=join)
 
 
 def carried_in(part, axis, combine, identity):
@@ -130,7 +137,7 @@
         "cnb,nq->cbq", normalized, frame_table(), precision=lax.Precision.HIGHEST
     ).astype(jnp.bfloat16)
     flattened = modulated.reshape(modulated.shape[0], FEEDS * 2 * MODF)
-    moved = lax.all_to_all(flattened, "shard", split_axis=1, concat_axis=0, tiled=True)
+    moved = trade_parts(flattened, "shard", 1, 0)
     local_beams = FEEDS // lax.axis_size("shard")
     gathered = moved.reshape(CHANS, local_beams, 2 * MODF)
     freq_major = jnp.transpose(gathered, (2, 0, 1))

time: 516 us -> 560 us (1.085)
  local copies, waits for them, and re-layouts: 131 us -> 175 us
    unnamed x16 -> x79, local copies, waits for them, and re-layouts: 0.93 us -> 41.9 us
    another operation x2 -> x4, local copies, waits for them, and re-layouts: 0.01 us -> 7.34 us  [the longest x1 6.67 us: shards(): gathered = moved.reshape(CHANS, local_beams, 2 * MODF)]
    all_to_all x3 -> x1, local copies, waits for them, and re-layouts: 10.3 us -> 3.34 us  [trade_parts(): blocks = lax.all_to_all(blocks, axis, split_axis=0, concat_axis=0)]
where the time goes in v1:
time: 560 us; the launch traced here: 554 us
  matrix products  217 us (39%)
  local copies, waits for them, and re-layouts  175 us (31%)
  waiting for transfers between devices  55.5 us (10%)
  other arithmetic  47.6 us (8%)
  loops' own time  27.1 us (5%)
  starting transfers between devices  22.3 us (4%)
  blocking collectives  8.44 us (2%)
    dot_general x7, matrix products, per_frequency(): lax.dot_general(sine_part, mod_imag, contract, preferred_element_type=jnp...  48.5 us
    dot_general x7, matrix products, per_frequency(): lax.dot_general(sine_part, mod_real, contract, preferred_element_type=jnp...  48.4 us
    dot_general x7, matrix products, per_frequency(): lax.dot_general(cosine_part, mod_real, contract, preferred_element_type=j...  48.1 us
    dot_general x7, matrix products, per_frequency(): lax.dot_general(cosine_part, mod_imag, contract, preferred_element_type=j...  48 us
    unnamed x79, local copies, waits for them, and re-layouts  41.9 us
    all_to_all x1, waiting for transfers between devices, shards(): lax.all_to_all(spectra, 'shard', split_axis=1, concat_axis=3, tiled=True)  39.9 us
    gather x2, local copies, waits for them, and re-layouts, form_beams(): jnp.take(calibrated, cell_feed, axis=3)  37.3 us
    another operation x1, loops' own time, dedisperse(): return lax.map(per_frequency, jnp.arange(MODF, dtype=jnp.int32))  27.1 us
  transfers between devices with their start and end apart: 2, of which 2 were waited for; matrix products, arithmetic and copies ran while one was open for 2% of the time, Pallas kernels for 0%

profile of v1, /device:TPU:1, one launch (start us, length us, event | category | flops | bytes accessed | tf_op | source)
XLA Modules:
  0.0 553.6 jit_solution(8334325291202764214)
XLA Ops:
  2.9 9.2 %multiply_convert_fusion = bf16[2048,512]{1,0:T(8,128)(2,1)} fusion(bf16[2048,2048]{1,0:T(8,128)(2,1)} %constant.189, bf16[512,2048]{1,0:T(8,128)(2,1)S(1)} %reshape_squeeze.3), kind=kOutput, calls=%fused_computation.43 | convolution fusion | flops 4297064448 | bytes 12582912 | tf_op jit(solution)/shard_map/dot_general | solution.py:119
  17.4 13.3 %all-to-all-start = ((bf16[2,1024,2,256]{3,2,0,1:T(2,128)(2,1)}), bf16[2,1024,2,256]{3,2,0,1:T(2,128)(2,1)S(1)}, u32[]{:S(2)}, u32[]{:S(2)}) async-start(bf16[2,1024,2,256]{3,2,0,1:T(2,128)(2,1)} %copy.40), calls=%async_computation | async-start | bytes 4194304 | tf_op jit(solution)/shard_map/all_to_all | solution.py:127
  30.8 4.8 scatter_custom_fusion
  40.5 39.9 %all-to-all-done = bf16[2,1024,2,256]{3,2,0,1:T(2,128)(2,1)S(1)} async-done(((bf16[2,1024,2,256]{3,2,0,1:T(2,128)(2,1)}), bf16[2,1024,2,256]{3,2,0,1:T(2,128)(2,1)S(1)}, u32[]{:S(2)}, u32[]{:S(2)}) %all-to-all-start) | async-done | bytes 2097184 | tf_op jit(solution)/shard_map/all_to_all | solution.py:127
  84.5 8.6 %slice.26 = f32[1,16,2,1024,16]{4,3,2,1,0:T(8,128)} reshape(f32[1,16,2,64,256]{4,3,2,1,0:T(8,128)S(1)} %copy.42) | data formatting | bytes 4194304 | tf_op jit(solution)/shard_map/slice | solution.py:67
  95.9 8.6 %slice.29 = f32[1,16,2,1024,16]{4,3,2,1,0:T(8,128)} reshape(f32[1,16,2,64,256]{4,3,2,1,0:T(8,128)S(1)} %copy.43) | data formatting | bytes 4194304 | tf_op jit(solution)/shard_map/slice | solution.py:67
  104.5 18.1 %multiply_subtract_fusion = (bf16[1,16,2,1024,16]{4,3,2,1,0:T(8,128)(2,1)}, bf16[1,16,2,1024,16]{4,3,2,1,0:T(8,128)(2,1)}) fusion(f32[1,16,2,1024,16]{4,3,2,1,0:T(8,128)} %slice.29, f32[1,16,2,1024,16]{4,3,2,1,0:T(8,128)} %slice.26, f32[16,1024]{1,0:T(8,128)S(1)} %get-tuple-element.203, f32[16,1024]{1,0:T(8,128)S(1)} %get-tuple-element.202), kind=kLoop, calls=%fused_computation.37 | loop fusion | flops 4194304 | bytes 6422528 | tf_op jit(solution)/shard_map/sub | solution.py:67
  122.5 6.7 %copy.44 = bf16[1,16,2,1024,16]{3,4,2,1,0:T(8,128)(2,1)S(1)} copy(bf16[1,16,2,1024,16]{4,3,2,1,0:T(8,128)(2,1)} %get-tuple-element.196) | data formatting | bytes 2097152 | tf_op jit(solution)/shard_map/sub | solution.py:67
  129.2 7.8 %copy.45 = bf16[1,16,2,1024,16]{3,4,2,1,0:T(8,128)(2,1)} copy(bf16[1,16,2,1024,16]{4,3,2,1,0:T(8,128)(2,1)} %get-tuple-element.197) | data formatting | bytes 2097152 | tf_op jit(solution)/shard_map/add | solution.py:68
  138.4 16.1 %copy.46 = bf16[2,16,2,1024,16]{4,1,3,2,0:T(8,128)(2,1)} copy(bf16[2,16,2,1024,16]{3,4,2,1,0:T(8,128)(2,1)S(1)} %pad_maximum_fusion) | data formatting | bytes 4194304 | tf_op jit(solution)/shard_map/stack | solution.py:69
  154.5 20.1 %gather_fusion = bf16[1024,2,16,2,16]{4,2,3,1,0:T(8,128)(2,1)} fusion(bf16[2,16,2,1024,16]{4,1,3,2,0:T(8,128)(2,1)} %copy.46, s32[1024]{0:T(1024)S(1)} %fusion.59), kind=kCustom, calls=%fused_computation | custom fusion | bytes 4198400 | tf_op jit(solution)/shard_map/jit(_take)/gather | solution.py:70
  174.7 17.1 %copy.47 = bf16[2,16,2,4,256,16]{4,5,0,3,2,1:T(8,128)(2,1)S(1)} copy(bf16[2,16,2,4,256,16]{5,1,2,0,4,3:T(8,128)(2,1)} %bitcast.366) | data formatting | bytes 4194304 | tf_op jit(solution)/shard_map/jit(_take)/gather | solution.py:70
  193.0 12.1 %fusion.25 = (f32[16]{0:T(128)S(1)}, f32[4,16,256,16]{2,0,3,1:T(4,128)S(1)}) fusion(f32[2,16,2,4,256,16]{4,5,3,2,1,0:T(8,128)S(1)} %convolution_bitcast_fusion, f32[1,4,2,4]{1,3,0,2:T(4,128)S(1)} %copy.38, f32[1,4,2,4]{1,3,0,2:T(4,128)S(1)} %copy.37), kind=kOutput, calls=%fused_computation.44 | convolution fusion | flops 103546928 | bytes 5243200 | tf_op jit(solution)/shard_map/bcpxwn,bxeu->ecpnuw/dot_general | solution.py:75
  205.3 8.4 %all-reduce.2 = (f32[64]{0:T(128)S(1)}, f32[64]{0:T(128)S(1)}) all-reduce(f32[64]{0:T(128)S(1)} %dynamic-update-slice, f32[64]{0:T(128)S(1)} %fusion.69), channel_id=2, replica_groups=mesh['section'=4,'shard'=64] {'section'}, use_global_device_ids=true, to_apply=%add | all-reduce | flops 128 | bytes 1024
  218.9 9.0 %reshape.240 = bf16[16,14336]{1,0:T(8,128)(2,1)S(1)} reshape(bf16[16,1024,14]{2,1,0:T(8,128)(2,1)} %copy.49) | data formatting | bytes 917504 | tf_op jit(solution)/shard_map/reshape | solution.py:139
  269.7 9.0 %all-to-all-start.1 = ((bf16[64,16,224]{2,1,0:T(8,128)(2,1)}), bf16[64,16,224]{2,1,0:T(8,128)(2,1)S(1)}, u32[]{:S(2)}, u32[]{:S(2)}) async-start(bf16[64,16,224]{2,1,0:T(8,128)(2,1)} %constant_dynamic-update-slice_fusion), calls=%async_computation.1 | async-start | bytes 1048576 | tf_op jit(solution)/shard_map/all_to_all | solution.py:21
  280.8 15.6 %all-to-all-done.1 = bf16[64,16,224]{2,1,0:T(8,128)(2,1)S(1)} async-done(((bf16[64,16,224]{2,1,0:T(8,128)(2,1)}), bf16[64,16,224]{2,1,0:T(8,128)(2,1)S(1)}, u32[]{:S(2)}, u32[]{:S(2)}) %all-to-all-start.1) | async-done | bytes 458784 | tf_op jit(solution)/shard_map/all_to_all | solution.py:21
  296.4 3.3 copy.50
  299.7 6.7 %reshape_reshape.3 = bf16[1024,16,14]{0,2,1:T(8,128)(2,1)S(1)} reshape(bf16[64,16,224]{1,0,2:T(8,128)(2,1)} %copy.50) | data formatting | bytes 917504 | tf_op jit(solution)/shard_map/reshape;reshape | solution.py:142
  306.7 246.6 %while.28 = (s32[]{:T(128)}, bf16[7,512,2,16]{1,3,2,0:T(8,128)(2,1)}, s32[7]{0:T(128)S(1)}, s32[1024,512]{1,0:T(8,128)}, bf16[14,1024,16]{1,2,0:T(8,128)(2,1)S(1...) while((s32[]{:T(128)}, bf16[7,512,2,16]{1,3,2,0:T(8,128)(2,1)}, s32[7]{0:T(128)S(1)}, ...), condition=%wide.region_6.7_spmd, body=%wide.region_5.6_spmd.sunk | while | flops 76611592 | bytes 13009633 | solution.py:102
  312.6 6.9 %fusion.98 = f32[512,16]{0,1:T(8,128)S(1)} fusion(f32[1024,512]{1,0:T(8,128)S(1)} %fusion.95, bf16[14,1024,16]{1,2,0:T(8,128)(2,1)S(1)} %get-tuple-element.336, s32[]{:T(128)S(6)} %select_n.175), kind=kOutput, calls=%fused_computation.19.clone.1 | convolution fusion | flops 17301504 | bytes 2162692 | tf_op jit(solution)/shard_map/while/body/eval_jaxpr/dot_general | solution.py:93
  320.8 6.9 %fusion.99 = f32[1,512,1,16]{1,3,2,0:T(8,128)S(1)} fusion(f32[512,16]{0,1:T(8,128)S(1)} %fusion.98, f32[1024,512]{1,0:T(8,128)S(1)} %fusion.95, bf16[14,1024,16]{1,2,0:T(8,128)(2,1)S(1)} %get-tuple-element.336, s32[]{:T(128)S(6)} %select_n.174), kind=kOutput, calls=%fused_computation.18.clone.1 | convolution fusion | flops 17309696 | bytes 2195460 | tf_op jit(solution)/shard_map/while/body/eval_jaxpr/dot_general | solution.py:95
  327.7 6.9 %fusion.96 = f32[512,16]{0,1:T(8,128)S(1)} fusion(f32[1024,512]{1,0:T(8,128)S(1)} %fusion.95, bf16[14,1024,16]{1,2,0:T(8,128)(2,1)S(1)} %get-tuple-element.336, s32[]{:T(128)S(6)} %select_n.174), kind=kOutput, calls=%fused_computation.20.clone.1 | convolution fusion | flops 17301504 | bytes 2162692 | tf_op jit(solution)/shard_map/while/body/eval_jaxpr/dot_general | solution.py:96
  334.5 6.9 %fusion.97 = f32[1,512,1,16]{1,3,2,0:T(8,128)S(1)} fusion(f32[512,16]{0,1:T(8,128)S(1)} %fusion.96, f32[1024,512]{1,0:T(8,128)S(1)} %fusion.95, bf16[14,1024,16]{1,2,0:T(8,128)(2,1)S(1)} %get-tuple-element.336, s32[]{:T(128)S(6)} %select_n.175), kind=kOutput, calls=%fused_computation.16.clone.1 | convolution fusion | flops 17309696 | bytes 2195460 | tf_op jit(solution)/shard_map/while/body/eval_jaxpr/dot_general | solution.py:98
  347.8 6.9 %fusion.98 = f32[512,16]{0,1:T(8,128)S(1)} fusion(f32[1024,512]{1,0:T(8,128)S(1)} %fusion.95, bf16[14,1024,16]{1,2,0:T(8,128)(2,1)S(1)} %get-tuple-element.336, s32[]{:T(128)S(6)} %select_n.175), kind=kOutput, calls=%fused_computation.19.clone.1 | convolution fusion | flops 17301504 | bytes 2162692 | tf_op jit(solution)/shard_map/while/body/eval_jaxpr/dot_general | solution.py:93
  356.0 6.9 %fusion.99 = f32[1,512,1,16]{1,3,2,0:T(8,128)S(1)} fusion(f32[512,16]{0,1:T(8,128)S(1)} %fusion.98, f32[1024,512]{1,0:T(8,128)S(1)} %fusion.95, bf16[14,1024,16]{1,2,0:T(8,128)(2,1)S(1)} %get-tuple-element.336, s32[]{:T(128)S(6)} %select_n.174), kind=kOutput, calls=%fused_computation.18.clone.1 | convolution fusion | flops 17309696 | bytes 2195460 | tf_op jit(solution)/shard_map/while/body/eval_jaxpr/dot_general | solution.py:95
  362.9 6.9 %fusion.96 = f32[512,16]{0,1:T(8,128)S(1)} fusion(f32[1024,512]{1,0:T(8,128)S(1)} %fusion.95, bf16[14,1024,16]{1,2,0:T(8,128)(2,1)S(1)} %get-tuple-element.336, s32[]{:T(128)S(6)} %select_n.174), kind=kOutput, calls=%fused_computation.20.clone.1 | convolution fusion | flops 17301504 | bytes 2162692 | tf_op jit(solution)/shard_map/while/body/eval_jaxpr/dot_general | solution.py:96
  369.7 6.9 %fusion.97 = f32[1,512,1,16]{1,3,2,0:T(8,128)S(1)} fusion(f32[512,16]{0,1:T(8,128)S(1)} %fusion.96, f32[1024,512]{1,0:T(8,128)S(1)} %fusion.95, bf16[14,1024,16]{1,2,0:T(8,128)(2,1)S(1)} %get-tuple-element.336, s32[]{:T(128)S(6)} %select_n.175), kind=kOutput, calls=%fused_computation.16.clone.1 | convolution fusion | flops 17309696 | bytes 2195460 | tf_op jit(solution)/shard_map/while/body/eval_jaxpr/dot_general | solution.py:98
  383.0 6.9 %fusion.98 = f32[512,16]{0,1:T(8,128)S(1)} fusion(f32[1024,512]{1,0:T(8,128)S(1)} %fusion.95, bf16[14,1024,16]{1,2,0:T(8,128)(2,1)S(1)} %get-tuple-element.336, s32[]{:T(128)S(6)} %select_n.175), kind=kOutput, calls=%fused_computation.19.clone.1 | convolution fusion | flops 17301504 | bytes 2162692 | tf_op jit(solution)/shard_map/while/body/eval_jaxpr/dot_general | solution.py:93
  391.1 6.9 %fusion.99 = f32[1,512,1,16]{1,3,2,0:T(8,128)S(1)} fusion(f32[512,16]{0,1:T(8,128)S(1)} %fusion.98, f32[1024,512]{1,0:T(8,128)S(1)} %fusion.95, bf16[14,1024,16]{1,2,0:T(8,128)(2,1)S(1)} %get-tuple-element.336, s32[]{:T(128)S(6)} %select_n.174), kind=kOutput, calls=%fused_computation.18.clone.1 | convolution fusion | flops 17309696 | bytes 2195460 | tf_op jit(solution)/shard_map/while/body/eval_jaxpr/dot_general | solution.py:95
  398.1 6.9 %fusion.96 = f32[512,16]{0,1:T(8,128)S(1)} fusion(f32[1024,512]{1,0:T(8,128)S(1)} %fusion.95, bf16[14,1024,16]{1,2,0:T(8,128)(2,1)S(1)} %get-tuple-element.336, s32[]{:T(128)S(6)} %select_n.174), kind=kOutput, calls=%fused_computation.20.clone.1 | convolution fusion | flops 17301504 | bytes 2162692 | tf_op jit(solution)/shard_map/while/body/eval_jaxpr/dot_general | solution.py:96
  404.9 6.9 %fusion.97 = f32[1,512,1,16]{1,3,2,0:T(8,128)S(1)} fusion(f32[512,16]{0,1:T(8,128)S(1)} %fusion.96, f32[1024,512]{1,0:T(8,128)S(1)} %fusion.95, bf16[14,1024,16]{1,2,0:T(8,128)(2,1)S(1)} %get-tuple-element.336, s32[]{:T(128)S(6)} %select_n.175), kind=kOutput, calls=%fused_computation.16.clone.1 | convolution fusion | flops 17309696 | bytes 2195460 | tf_op jit(solution)/shard_map/while/body/eval_jaxpr/dot_general | solution.py:98
  418.2 6.9 %fusion.98 = f32[512,16]{0,1:T(8,128)S(1)} fusion(f32[1024,512]{1,0:T(8,128)S(1)} %fusion.95, bf16[14,1024,16]{1,2,0:T(8,128)(2,1)S(1)} %get-tuple-element.336, s32[]{:T(128)S(6)} %select_n.175), kind=kOutput, calls=%fused_computation.19.clone.1 | convolution fusion | flops 17301504 | bytes 2162692 | tf_op jit(solution)/shard_map/while/body/eval_jaxpr/dot_general | solution.py:93
  426.3 6.9 %fusion.99 = f32[1,512,1,16]{1,3,2,0:T(8,128)S(1)} fusion(f32[512,16]{0,1:T(8,128)S(1)} %fusion.98, f32[1024,512]{1,0:T(8,128)S(1)} %fusion.95, bf16[14,1024,16]{1,2,0:T(8,128)(2,1)S(1)} %get-tuple-element.336, s32[]{:T(128)S(6)} %select_n.174), kind=kOutput, calls=%fused_computation.18.clone.1 | convolution fusion | flops 17309696 | bytes 2195460 | tf_op jit(solution)/shard_map/while/body/eval_jaxpr/dot_general | solution.py:95
  433.3 6.9 %fusion.96 = f32[512,16]{0,1:T(8,128)S(1)} fusion(f32[1024,512]{1,0:T(8,128)S(1)} %fusion.95, bf16[14,1024,16]{1,2,0:T(8,128)(2,1)S(1)} %get-tuple-element.336, s32[]{:T(128)S(6)} %select_n.174), kind=kOutput, calls=%fused_computation.20.clone.1 | convolution fusion | flops 17301504 | bytes 2162692 | tf_op jit(solution)/shard_map/while/body/eval_jaxpr/dot_general | solution.py:96
  440.1 6.9 %fusion.97 = f32[1,512,1,16]{1,3,2,0:T(8,128)S(1)} fusion(f32[512,16]{0,1:T(8,128)S(1)} %fusion.96, f32[1024,512]{1,0:T(8,128)S(1)} %fusion.95, bf16[14,1024,16]{1,2,0:T(8,128)(2,1)S(1)} %get-tuple-element.336, s32[]{:T(128)S(6)} %select_n.175), kind=kOutput, calls=%fused_computation.16.clone.1 | convolution fusion | flops 17309696 | bytes 2195460 | tf_op jit(solution)/shard_map/while/body/eval_jaxpr/dot_general | solution.py:98
  453.4 6.9 %fusion.98 = f32[512,16]{0,1:T(8,128)S(1)} fusion(f32[1024,512]{1,0:T(8,128)S(1)} %fusion.95, bf16[14,1024,16]{1,2,0:T(8,128)(2,1)S(1)} %get-tuple-element.336, s32[]{:T(128)S(6)} %select_n.175), kind=kOutput, calls=%fused_computation.19.clone.1 | convolution fusion | flops 17301504 | bytes 2162692 | tf_op jit(solution)/shard_map/while/body/eval_jaxpr/dot_general | solution.py:93
  461.5 6.9 %fusion.99 = f32[1,512,1,16]{1,3,2,0:T(8,128)S(1)} fusion(f32[512,16]{0,1:T(8,128)S(1)} %fusion.98, f32[1024,512]{1,0:T(8,128)S(1)} %fusion.95, bf16[14,1024,16]{1,2,0:T(8,128)(2,1)S(1)} %get-tuple-element.336, s32[]{:T(128)S(6)} %select_n.174), kind=kOutput, calls=%fused_computation.18.clone.1 | convolution fusion | flops 17309696 | bytes 2195460 | tf_op jit(solution)/shard_map/while/body/eval_jaxpr/dot_general | solution.py:95
  468.5 6.9 %fusion.96 = f32[512,16]{0,1:T(8,128)S(1)} fusion(f32[1024,512]{1,0:T(8,128)S(1)} %fusion.95, bf16[14,1024,16]{1,2,0:T(8,128)(2,1)S(1)} %get-tuple-element.336, s32[]{:T(128)S(6)} %select_n.174), kind=kOutput, calls=%fused_computation.20.clone.1 | convolution fusion | flops 17301504 | bytes 2162692 | tf_op jit(solution)/shard_map/while/body/eval_jaxpr/dot_general | solution.py:96
  475.3 6.9 %fusion.97 = f32[1,512,1,16]{1,3,2,0:T(8,128)S(1)} fusion(f32[512,16]{0,1:T(8,128)S(1)} %fusion.96, f32[1024,512]{1,0:T(8,128)S(1)} %fusion.95, bf16[14,1024,16]{1,2,0:T(8,128)(2,1)S(1)} %get-tuple-element.336, s32[]{:T(128)S(6)} %select_n.175), kind=kOutput, calls=%fused_computation.16.clone.1 | convolution fusion | flops 17309696 | bytes 2195460 | tf_op jit(solution)/shard_map/while/body/eval_jaxpr/dot_general | solution.py:98
  488.6 6.9 %fusion.98 = f32[512,16]{0,1:T(8,128)S(1)} fusion(f32[1024,512]{1,0:T(8,128)S(1)} %fusion.95, bf16[14,1024,16]{1,2,0:T(8,128)(2,1)S(1)} %get-tuple-element.336, s32[]{:T(128)S(6)} %select_n.175), kind=kOutput, calls=%fused_computation.19.clone.1 | convolution fusion | flops 17301504 | bytes 2162692 | tf_op jit(solution)/shard_map/while/body/eval_jaxpr/dot_general | solution.py:93
  496.7 6.9 %fusion.99 = f32[1,512,1,16]{1,3,2,0:T(8,128)S(1)} fusion(f32[512,16]{0,1:T(8,128)S(1)} %fusion.98, f32[1024,512]{1,0:T(8,128)S(1)} %fusion.95, bf16[14,1024,16]{1,2,0:T(8,128)(2,1)S(1)} %get-tuple-element.336, s32[]{:T(128)S(6)} %select_n.174), kind=kOutput, calls=%fused_computation.18.clone.1 | convolution fusion | flops 17309696 | bytes 2195460 | tf_op jit(solution)/shard_map/while/body/eval_jaxpr/dot_general | solution.py:95
  503.6 6.9 %fusion.96 = f32[512,16]{0,1:T(8,128)S(1)} fusion(f32[1024,512]{1,0:T(8,128)S(1)} %fusion.95, bf16[14,1024,16]{1,2,0:T(8,128)(2,1)S(1)} %get-tuple-element.336, s32[]{:T(128)S(6)} %select_n.174), kind=kOutput, calls=%fused_computation.20.clone.1 | convolution fusion | flops 17301504 | bytes 2162692 | tf_op jit(solution)/shard_map/while/body/eval_jaxpr/dot_general | solution.py:96
  510.5 6.9 %fusion.97 = f32[1,512,1,16]{1,3,2,0:T(8,128)S(1)} fusion(f32[512,16]{0,1:T(8,128)S(1)} %fusion.96, f32[1024,512]{1,0:T(8,128)S(1)} %fusion.95, bf16[14,1024,16]{1,2,0:T(8,128)(2,1)S(1)} %get-tuple-element.336, s32[]{:T(128)S(6)} %select_n.175), kind=kOutput, calls=%fused_computation.16.clone.1 | convolution fusion | flops 17309696 | bytes 2195460 | tf_op jit(solution)/shard_map/while/body/eval_jaxpr/dot_general | solution.py:98
  523.7 6.9 %fusion.98 = f32[512,16]{0,1:T(8,128)S(1)} fusion(f32[1024,512]{1,0:T(8,128)S(1)} %fusion.95, bf16[14,1024,16]{1,2,0:T(8,128)(2,1)S(1)} %get-tuple-element.336, s32[]{:T(128)S(6)} %select_n.175), kind=kOutput, calls=%fused_computation.19.clone.1 | convolution fusion | flops 17301504 | bytes 2162692 | tf_op jit(solution)/shard_map/while/body/eval_jaxpr/dot_general | solution.py:93
  531.9 6.9 %fusion.99 = f32[1,512,1,16]{1,3,2,0:T(8,128)S(1)} fusion(f32[512,16]{0,1:T(8,128)S(1)} %fusion.98, f32[1024,512]{1,0:T(8,128)S(1)} %fusion.95, bf16[14,1024,16]{1,2,0:T(8,128)(2,1)S(1)} %get-tuple-element.336, s32[]{:T(128)S(6)} %select_n.174), kind=kOutput, calls=%fused_computation.18.clone.1 | convolution fusion | flops 17309696 | bytes 2195460 | tf_op jit(solution)/shard_map/while/body/eval_jaxpr/dot_general | solution.py:95
  538.8 6.9 %fusion.96 = f32[512,16]{0,1:T(8,128)S(1)} fusion(f32[1024,512]{1,0:T(8,128)S(1)} %fusion.95, bf16[14,1024,16]{1,2,0:T(8,128)(2,1)S(1)} %get-tuple-element.336, s32[]{:T(128)S(6)} %select_n.174), kind=kOutput, calls=%fused_computation.20.clone.1 | convolution fusion | flops 17301504 | bytes 2162692 | tf_op jit(solution)/shard_map/while/body/eval_jaxpr/dot_general | solution.py:96
  545.7 6.9 %fusion.97 = f32[1,512,1,16]{1,3,2,0:T(8,128)S(1)} fusion(f32[512,16]{0,1:T(8,128)S(1)} %fusion.96, f32[1024,512]{1,0:T(8,128)S(1)} %fusion.95, bf16[14,1024,16]{1,2,0:T(8,128)(2,1)S(1)} %get-tuple-element.336, s32[]{:T(128)S(6)} %select_n.175), kind=kOutput, calls=%fused_computation.16.clone.1 | convolution fusion | flops 17309696 | bytes 2195460 | tf_op jit(solution)/shard_map/while/body/eval_jaxpr/dot_general | solution.py:98
  (142 shorter events, 97.8 us)
Async XLA Ops:
  17.4 13.3 %copy-start.2 = (bf16[2,16,1024]{2,1,0:T(8,128)(2,1)S(1)}, bf16[2,16,1024]{2,1,0:T(8,128)(2,1)}, u32[]{:S(2)}) copy-start(bf16[2,16,1024]{2,1,0:T(8,128)(2,1)} %param.11) | copy-start | bytes 196612
  17.4 13.3 %copy-start.3 = (s32[1024]{0:T(1024)S(1)}, s32[1024]{0:T(1024)}, u32[]{:S(2)}) copy-start(s32[1024]{0:T(1024)} %param.12) | copy-start | bytes 12292
  17.4 18.5 %copy-start.5 = (u32[256]{0:T(256)S(1)}, u32[256]{0:T(256)}, u32[]{:S(2)}) copy-start(u32[256]{0:T(256)} %constant.192) | copy-start | bytes 3076
  17.4 19.9 %copy-start.4 = (f32[16]{0:T(128)S(1)}, f32[16]{0:T(128)}, u32[]{:S(2)}) copy-start(f32[16]{0:T(128)} %param.13) | copy-start | bytes 196
  17.4 63.0 %all-to-all-start = ((bf16[2,1024,2,256]{3,2,0,1:T(2,128)(2,1)}), bf16[2,1024,2,256]{3,2,0,1:T(2,128)(2,1)S(1)}, u32[]{:S(2)}, u32[]{:S(2)}) async-start(bf16[2,1024,2,256]{3,2,0,1:T(2,128)(2,1)} %copy.40), calls=%async_computation | async-start | bytes 4194304 | tf_op jit(solution)/shard_map/all_to_all | solution.py:127
  174.6 17.1 %copy-start.1 = (bf16[1,256,2,256]{3,1,0,2:T(8,128)(2,1)S(1)}, bf16[1,256,2,256]{3,1,0,2:T(8,128)(2,1)}, u32[]{:S(2)}) copy-start(bf16[1,256,2,256]{3,1,0,2:T(8,128)(2,1)} %get-tuple-element.201) | copy-start | bytes 786436
  228.0 50.7 %copy-start = (s32[1024,512]{1,0:T(8,128)S(1)}, s32[1024,512]{1,0:T(8,128)}, u32[]{:S(2)}) copy-start(s32[1024,512]{1,0:T(8,128)} %param.14) | copy-start | bytes 6291460
  269.7 26.7 %all-to-all-start.1 = ((bf16[64,16,224]{2,1,0:T(8,128)(2,1)}), bf16[64,16,224]{2,1,0:T(8,128)(2,1)S(1)}, u32[]{:S(2)}, u32[]{:S(2)}) async-start(bf16[64,16,224]{2,1,0:T(8,128)(2,1)} %constant_dynamic-update-slice_fusion), calls=%async_computation.1 | async-start | bytes 1048576 | tf_op jit(solution)/shard_map/all_to_all | solution.py:21
